TPU v7x, 32 devices: a whole 2x2x4 slice. The times are simulated.
32 devices in a mesh: src: 16 (over z, x, core), tgt: 2 (over y).
Axes of the slice: x: 2, y: 2, z: 4, core: 2. Of those that a mesh axis runs over, the one named last changes fastest.
Arguments:
- source_embed: bfloat16 [128, 65536], P(None, 'src'), may hold values from -1 to 1
- target_embed: bfloat16 [128, 1024], P(None, 'tgt'), may hold values from -1 to 1
- source_expr: bfloat16 [128, 65536], P(None, 'src'), may hold values from -0.5390625 to 0.5390625
- target_expr: bfloat16 [128, 1024], P(None, 'tgt'), may hold values from -0.5390625 to 0.5390625
- current_plan: bfloat16 [65536, 1024], P('src', 'tgt'), as said below
- source_mass: float32 [65536], P('src'), may hold values from 0.25 to 4
- target_mass: float32 [1024], P('tgt'), may hold values from 0.25 to 4
- source_potential: float32 [65536], P('src'), may hold values from -16 to 16
- target_genes: bfloat16 [1024, 256], P('tgt'), may hold values from -6 to 6
Outputs:
- imputed: bfloat16 [65536, 256], P(('src', 'tgt'))
Inputs may be any that keep to these rules, and one draw needn't show every extreme that they name: Every entry of current_plan is positive.
All inputs are finite; a program needn't handle non-finite values.
Results may differ from a plain program's by a relative error of at most 0.014.
Values may be sent and summed in bfloat16 or wider, within the bound.
A program may use at most 64 MiB of HBM per device.

v0:
```python
import jax
import jax.numpy as jnp
from jax import lax
from jax.sharding import PartitionSpec as P

ITERS = 2
epsilon = 0.05
geometry_weight = 4.0


def joined(value, axis, join):
    pieces = jax.tree.map(lambda part: lax.all_gather(part, axis), value)
    head = jax.tree.map(lambda part: part[0], pieces)
    tail = jax.tree.map(lambda part: part[1:], pieces)
    so_far, _ = lax.scan(lambda so_far, piece: (join(so_far, piece), None), head, tail)
    return so_far


def factors(embed):
    widened = embed.astype(jnp.float32)
    squares = jnp.sum(widened * widened, axis=0)
    unit_row = jnp.ones_like(squares)
    left_factor = jnp.concatenate([squares[None, :], unit_row[None, :], -2.0 * widened], axis=0)
    right_factor = jnp.concatenate([unit_row[None, :], squares[None, :], widened], axis=0)
    return (left_factor, right_factor)


def combine_pair(earlier, later):
    maximum = jnp.maximum(earlier[0], later[0])
    return (
        maximum,
        earlier[1] * jnp.exp(earlier[0] - maximum) + later[1] * jnp.exp(later[0] - maximum),
    )


def column_logsum(scores):
    local_max = jnp.max(scores, axis=0)
    local_sum = jnp.sum(jnp.exp(scores - local_max[None, :]), axis=0)
    maximum, totals = joined((local_max, local_sum), "src", combine_pair)
    return maximum + jnp.log(totals)


def row_logsum(scores):
    local_max = jnp.max(scores, axis=1)
    local_sum = jnp.sum(jnp.exp(scores - local_max[:, None]), axis=1)
    maximum, totals = joined((local_max, local_sum), "tgt", combine_pair)
    return maximum + jnp.log(totals)


def shards(
    source_embed,
    target_embed,
    source_expr,
    target_expr,
    current_plan,
    source_mass,
    target_mass,
    source_potential,
    target_genes,
):
    highest = lax.Precision.HIGHEST
    spot_rows = source_embed.shape[1]
    spot_cols = target_embed.shape[1]
    total_pairs = float(spot_rows * lax.axis_size("src") * spot_cols * lax.axis_size("tgt"))
    left_src, right_src = factors(source_embed)
    left_tgt, right_tgt = factors(target_embed)
    projected = jnp.dot(
        current_plan.astype(jnp.float32),
        right_tgt.T,
        precision=highest,
        preferred_element_type=jnp.float32,
    )
    partial_core = jnp.dot(
        right_src, projected, precision=highest, preferred_element_type=jnp.float32
    )
    core_matrix = lax.psum(partial_core, ("src", "tgt")) / total_pairs
    geometry_right = jnp.dot(
        core_matrix, left_tgt, precision=highest, preferred_element_type=jnp.float32
    )
    geometry = lax.dot_general(
        left_src,
        geometry_right,
        (((0,), (0,)), ((), ())),
        precision=highest,
        preferred_element_type=jnp.float32,
    )
    feature = lax.dot_general(
        source_expr, target_expr, (((0,), (0,)), ((), ())), preferred_element_type=jnp.float32
    )
    cost_tile = -2.0 * (feature + geometry_weight * geometry)
    log_src = jnp.log(source_mass)
    log_tgt = jnp.log(target_mass)
    potential_src = source_potential
    potential_tgt = jnp.zeros((spot_cols,), jnp.float32)
    for iteration in range(ITERS):
        potential_tgt = epsilon * log_tgt - epsilon * column_logsum(
            (potential_src[:, None] - cost_tile) / epsilon
        )
        potential_src = epsilon * log_src - epsilon * row_logsum(
            (potential_tgt[None, :] - cost_tile) / epsilon
        )
    weights = jnp.exp(
        (potential_src[:, None] + potential_tgt[None, :] - cost_tile) / epsilon
    ).astype(jnp.bfloat16)
    row_share = spot_rows // lax.axis_size("tgt")
    row_offset = lax.axis_index("tgt") * row_share
    mass_rows = lax.dynamic_slice_in_dim(source_mass, row_offset, row_share)
    numerator = lax.psum_scatter(
        jnp.dot(weights, target_genes, preferred_element_type=jnp.float32).astype(jnp.bfloat16),
        "tgt",
        scatter_dimension=0,
        tiled=True,
    ).astype(jnp.float32)
    return (numerator / mass_rows[:, None]).astype(jnp.bfloat16)


def solution(mesh):
    return jax.shard_map(
        shards,
        mesh=mesh,
        in_specs=(
            P(None, "src"),
            P(None, "tgt"),
            P(None, "src"),
            P(None, "tgt"),
            P("src", "tgt"),
            P("src"),
            P("tgt"),
            P("src"),
            P("tgt", None),
        ),
        out_specs=P(("src", "tgt"), None),
        check_vma=False,
    )
```

profile of v0, /device:TPU:0, one launch (start us, length us, event | category | flops | bytes accessed | tf_op | source)
XLA Modules:
  0.0 319.4 jit_solution(5949856165096476949)
XLA Ops:
  6.5 0.0 copy-start
  6.5 0.0 all-reduce.2.cloned.1.call-start
  6.5 1.1 multiply_reduce_fusion.1
  7.7 1.2 convert_element_type.20
  8.9 1.6 broadcast_multiply_fusion
  10.4 1.4 convert_element_type.19
  11.9 0.0 copy-done.3
  11.9 4.3 %fusion.18 = f32[130,4096]{1,0:T(8,128)S(1)} fusion(bf16[4096,512]{1,0:T(8,128)(2,1)S(1)} %copy-done.3, f32[128,512]{1,0:T(8,128)S(1)} %convert_element_type.20, f32[1,512]{1,0:T(1,128)S(1)} %bitcast.56, f32[1,512]{1,0:T(1,128)S(1)} %broadcast.34), kind=kOutput, calls=%fused_computation.38 | convolution fusion | flops 3271690240 | bytes 6590464 | tf_op jit(solution)/shard_map/dot_general | solution.py:67
  16.2 2.8 fusion.12
  19.0 0.0 all-reduce.2.cloned.1.call-update
  19.0 0.2 reduce-scatter.2.cloned.1.call-start
  19.3 0.0 copy-done
  19.3 5.4 %fusion.50 = f32[4096,512]{1,0:T(8,128)} fusion(bf16[128,4096]{1,0:T(8,128)(2,1)S(1)} %copy-done, bf16[128,512]{1,0:T(8,128)(2,1)} %param.16), kind=kOutput, calls=%fused_computation.86 | convolution fusion | flops 536870912 | bytes 9568256 | tf_op jit(solution)/shard_map/dot_general | solution.py:87
  24.7 117.4 %all-reduce.2.cloned.1.call-done = f32[130,130]{1,0:T(8,128)} async-done(((f32[130,130]{1,0:T(8,128)}), f32[130,130]{1,0:T(8,128)}) %all-reduce.2.cloned.1.call-update) | async-done | bytes 67616 | tf_op jit(solution)/shard_map/psum | solution.py:76
  142.1 1.3 fusion.24
  143.4 0.0 copy-done.5
  143.4 11.4 %fusion = (f32[512]{0:T(512)S(1)}, f32[4096,512]{1,0:T(8,128)S(1)}) fusion(f32[4096]{0:T(1024)S(1)} %copy-done.5, f32[4096,512]{1,0:T(8,128)} %fusion.50, f32[130,512]{1,0:T(8,128)S(1)} %fusion.24, f32[128,4096]{1,0:T(8,128)S(1)} %get-tuple-element.123, f32[1,4096]{1,0:T(1,128)S(1)} %broadcast.33, f32[1,4096]{1,0:T(1,128)S(1)} %bitcast.47), kind=kOutput, calls=%fused_computation.16 | convolution fusion | flops 3285204480 | bytes 19191808 | tf_op jit(solution)/shard_map/dot_general | solution.py:80
  154.8 0.0 copy-start.1
  154.8 0.0 copy-start.6
  154.8 3.2 %copy-done.1 = f32[4096,512]{1,0:T(8,128)} copy-done((f32[4096,512]{1,0:T(8,128)}, f32[4096,512]{1,0:T(8,128)S(1)}, u32[]{:S(2)}) %copy-start.1) | copy-done | bytes 8388632
  158.0 1.8 exponential_reduce_fusion.3
  159.8 22.9 %all-gather.9 = f32[16,1,512]{2,1,0:T(1,128)S(1)} all-gather(f32[1,1,512]{2,1,0:T(1,128)S(1)} %bitcast.61), channel_id=3, replica_groups=mesh['src'=16,'tgt'=2] {'src'}, dimensions={0}, use_global_device_ids=true | all-gather | bytes 34816 | tf_op jit(solution)/shard_map/all_gather | solution.py:12
  182.7 17.5 %all-gather.8 = f32[16,1,512]{2,1,0:T(1,128)S(1)} all-gather(f32[1,1,512]{2,1,0:T(1,128)S(1)} %bitcast.58), channel_id=2, replica_groups=mesh['src'=16,'tgt'=2] {'src'}, dimensions={0}, use_global_device_ids=true | all-gather | bytes 34816 | tf_op jit(solution)/shard_map/all_gather | solution.py:12
  200.2 0.8 while.4
  201.0 0.0 copy-start.2
  201.0 0.0 copy-done.6
  201.0 0.0 copy-start.4
  201.1 4.4 %fusion.1 = f32[4096]{0:T(1024)S(1)} fusion(f32[4096,512]{1,0:T(8,128)} %copy-done.1, f32[512]{0:T(512)S(1)} %multiply_subtract_fusion.1), kind=kLoop, calls=%fused_computation.17 | loop fusion | flops 6287360 | bytes 8407040 | tf_op jit(solution)/shard_map/reduce_max | solution.py:44
  205.5 1.3 copy-done.2
  206.8 2.2 exponential_reduce_fusion.2
  209.0 4.4 %all-gather.2 = f32[8192]{0:T(1024)S(1)} all-gather(f32[4096]{0:T(1024)S(1)} %fusion.1), channel_id=4, replica_groups=mesh['src'=16,'tgt'=2] {'tgt'}, dimensions={0}, use_global_device_ids=true | all-gather | bytes 49152 | tf_op jit(solution)/shard_map/all_gather | solution.py:12
  213.4 4.4 %all-gather.3 = f32[8192]{0:T(1024)S(1)} all-gather(f32[4096]{0:T(1024)S(1)} %exponential_reduce_fusion.2), channel_id=5, replica_groups=mesh['src'=16,'tgt'=2] {'tgt'}, dimensions={0}, use_global_device_ids=true | all-gather | bytes 49152 | tf_op jit(solution)/shard_map/all_gather | solution.py:12
  217.8 1.0 fusion.2
  218.8 1.8 exponential_reduce_fusion.1
  220.6 18.9 %all-gather.11 = f32[16,1,512]{2,1,0:T(1,128)S(1)} all-gather(f32[1,1,512]{2,1,0:T(1,128)S(1)} %bitcast.60), channel_id=7, replica_groups=mesh['src'=16,'tgt'=2] {'src'}, dimensions={0}, use_global_device_ids=true | all-gather | bytes 34816 | tf_op jit(solution)/shard_map/all_gather | solution.py:12
  239.5 17.7 %all-gather.10 = f32[16,1,512]{2,1,0:T(1,128)S(1)} all-gather(f32[1,1,512]{2,1,0:T(1,128)S(1)} %bitcast.59), channel_id=6, replica_groups=mesh['src'=16,'tgt'=2] {'src'}, dimensions={0}, use_global_device_ids=true | all-gather | bytes 34816 | tf_op jit(solution)/shard_map/all_gather | solution.py:12
  257.2 0.8 while.5
  258.1 0.0 slice-start
  258.1 0.0 copy-start.7
  258.1 4.4 %fusion.3 = f32[4096]{0:T(1024)S(1)} fusion(f32[4096,512]{1,0:T(8,128)} %copy-done.1, f32[512]{0:T(512)S(1)} %multiply_subtract_fusion), kind=kLoop, calls=%fused_computation.19 | loop fusion | flops 6287360 | bytes 8407040 | tf_op jit(solution)/shard_map/reduce_max | solution.py:44
  262.5 0.0 slice-start.1
  262.5 5.1 %exponential_reduce_fusion = f32[4096]{0:T(1024)S(1)} fusion(f32[4096,512]{1,0:T(8,128)} %copy-done.1, f32[4096]{0:T(1024)S(1)} %fusion.3, f32[512]{0:T(512)S(1)} %multiply_subtract_fusion), kind=kLoop, calls=%fused_computation.7 | loop fusion | flops 8384512 | bytes 8423424 | tf_op jit(solution)/shard_map/reduce_sum | solution.py:45
  267.6 4.4 %all-gather.6 = f32[8192]{0:T(1024)S(1)} all-gather(f32[4096]{0:T(1024)S(1)} %fusion.3), channel_id=8, replica_groups=mesh['src'=16,'tgt'=2] {'tgt'}, dimensions={0}, use_global_device_ids=true | all-gather | bytes 49152 | tf_op jit(solution)/shard_map/all_gather | solution.py:12
  272.0 4.4 %all-gather.7 = f32[8192]{0:T(1024)S(1)} all-gather(f32[4096]{0:T(1024)S(1)} %exponential_reduce_fusion), channel_id=9, replica_groups=mesh['src'=16,'tgt'=2] {'tgt'}, dimensions={0}, use_global_device_ids=true | all-gather | bytes 49152 | tf_op jit(solution)/shard_map/all_gather | solution.py:12
  276.5 3.2 %convolution_convert_fusion = bf16[4096,256]{1,0:T(8,128)(2,1)} fusion(bf16[512,256]{1,0:T(8,128)(2,1)S(1)} %copy-done.7, f32[4096,512]{1,0:T(8,128)S(1)} %bitcast.41, f32[4096]{0:T(1024)S(1)} %fusion.36, f32[512]{0:T(512)S(1)} %multiply_subtract_fusion), kind=kOutput, calls=%fused_computation.20 | convolution fusion | flops 1083179008 | bytes 10766336 | tf_op jit(solution)/shard_map/dot_general | solution.py:109
  279.7 0.0 reduce-scatter.2.cloned.1.call-update
  279.8 30.3 %reduce-scatter.2.cloned.1.call-done = bf16[2048,256]{1,0:T(8,128)(2,1)} async-done(((bf16[4096,256]{1,0:T(8,128)(2,1)}), bf16[2048,256]{1,0:T(8,128)(2,1)}) %reduce-scatter.2.cloned.1.call-update) | async-done | bytes 1048592 | tf_op jit(solution)/shard_map/reduce_scatter | solution.py:108
  310.1 2.5 divide_convert_fusion
  (86 shorter events, 1.1 us)
Async XLA Ops:
  6.5 12.7 %copy-start = (bf16[128,4096]{1,0:T(8,128)(2,1)S(1)}, bf16[128,4096]{1,0:T(8,128)(2,1)}, u32[]{:S(2)}) copy-start(bf16[128,4096]{1,0:T(8,128)(2,1)} %param.15) | copy-start | bytes 3145732
  6.5 135.5 %all-reduce.2.cloned.1.call-start = ((), (), s32[]{:S(2)}) async-start(), calls=%async_computation.1 | async-start | bytes 278528 | tf_op jit(solution)/shard_map/psum | solution.py:76
  6.5 5.4 %copy-start.3 = (bf16[4096,512]{1,0:T(8,128)(2,1)S(1)}, bf16[4096,512]{1,0:T(8,128)(2,1)}, u32[]{:S(2)}) copy-start(bf16[4096,512]{1,0:T(8,128)(2,1)} %param.17) | copy-start | bytes 12582916
  19.0 124.4 %copy-start.5 = (f32[4096]{0:T(1024)S(1)}, f32[4096]{0:T(1024)}, u32[]{:S(2)}) copy-start(f32[4096]{0:T(1024)} %param.20) | copy-start | bytes 49156
  19.0 291.0 %reduce-scatter.2.cloned.1.call-start = ((), (), s32[]{:S(2)}) async-start(), calls=%async_computation.2 | async-start | bytes 3145728 | tf_op jit(solution)/shard_map/reduce_scatter | solution.py:108
  154.8 3.2 %copy-start.1 = (f32[4096,512]{1,0:T(8,128)}, f32[4096,512]{1,0:T(8,128)S(1)}, u32[]{:S(2)}) copy-start(f32[4096,512]{1,0:T(8,128)S(1)} %get-tuple-element.128) | copy-start | bytes 25165828
  154.8 46.2 %copy-start.6 = (f32[512]{0:T(512)S(1)}, f32[512]{0:T(512)}, u32[]{:S(2)}) copy-start(f32[512]{0:T(512)} %param.19) | copy-start | bytes 6148
  201.0 5.8 %copy-start.2 = (f32[4096,512]{1,0:T(8,128)S(1)}, f32[4096,512]{1,0:T(8,128)}, u32[]{:S(2)}) copy-start(f32[4096,512]{1,0:T(8,128)} %copy-done.1) | copy-start | bytes 25165828
  201.0 16.8 %copy-start.4 = (f32[4096]{0:T(1024)S(1)}, f32[4096]{0:T(1024)}, u32[]{:S(2)}) copy-start(f32[4096]{0:T(1024)} %param.18) | copy-start | bytes 49156
  258.1 18.4 %slice-start = ((s8[8388608]{0:T(1024)(128)(4,1)}), s8[4194304]{0:T(1024)(128)(4,1)S(1)}, s32[]{:S(2)}) async-start(s8[8388608]{0:T(1024)(128)(4,1)} %bitcast.40), calls=%async_computation.3 | async-start | bytes 8388608
  258.1 18.4 %copy-start.7 = (bf16[512,256]{1,0:T(8,128)(2,1)S(1)}, bf16[512,256]{1,0:T(8,128)(2,1)}, u32[]{:S(2)}) copy-start(bf16[512,256]{1,0:T(8,128)(2,1)} %param.21) | copy-start | bytes 786436
  262.5 14.0 %slice-start.1 = ((s8[8388608]{0:T(1024)(128)(4,1)}), s8[4194304]{0:T(1024)(128)(4,1)S(1)}, s32[]{:S(2)}) async-start(s8[8388608]{0:T(1024)(128)(4,1)} %bitcast.40), calls=%async_computation.4 | async-start | bytes 8388608
Sparse Core Ops, SparseCore 0:
  19.1 122.8 all-reduce.1
  279.9 30.1 reduce-scatter.1
where the time goes:
time: 320 us; the launch traced here: 319 us
  waiting for transfers between devices  148 us (46%)
  blocking collectives  94.5 us (30%)
  other arithmetic  29.3 us (9%)
  matrix products  28.4 us (9%)
  between operations  13.7 us (4%)
  local copies, waits for them, and re-layouts  4.93 us (2%)
    psum x1, waiting for transfers between devices, shards(): core_matrix = lax.psum(partial_core, ('src', 'tgt')) / total_pairs  117 us
    all_gather x8, blocking collectives, joined(): pieces = jax.tree.map(lambda part: lax.all_gather(part, axis), value)  94.5 us
    reduce_scatter x1, waiting for transfers between devices, shards(): lax.psum_scatter(jnp.dot(weights, target_genes, preferred_element_type=jn...  30.3 us
    dot_general x1, matrix products, shards(): lax.dot_general(left_src, geometry_right, (((0,), (0,)), ((), ())), preci...  11.4 us
    reduce_max x2, other arithmetic, row_logsum(): local_max = jnp.max(scores, axis=1)  8.87 us
    reduce_sum x2, other arithmetic, row_logsum(): local_sum = jnp.sum(jnp.exp(scores - local_max[:, None]), axis=1)  7.28 us
  transfers between devices with their start and end apart: 2, of which 2 were waited for; matrix products, arithmetic and copies ran while one was open for 2% of the time, Pallas kernels for 0%

commit v1 on v0

--- a/solution.py
+++ b/solution.py
@@ -2,6 +2,7 @@
 import jax.numpy as jnp
 from jax import lax
 from jax.sharding import PartitionSpec as P
+from jax.lax import all_gather
 
 ITERS = 2
 epsilon = 0.05
@@ -73,7 +74,7 @@
     partial_core = jnp.dot(
         right_src, projected, precision=highest, preferred_element_type=jnp.float32
     )
-    core_matrix = lax.psum(partial_core, ("src", "tgt")) / total_pairs
+    core_matrix = all_gather(partial_core, axis_name=("src", "tgt")).sum(axis=0) / total_pairs
     geometry_right = jnp.dot(
         core_matrix, left_tgt, precision=highest, preferred_element_type=jnp.float32
     )

time: 320 us -> 261 us (0.82)
  waiting for transfers between devices: 148 us -> 90.6 us
    psum x1 -> x0, waiting for transfers between devices: 117 us -> none  [shards(): core_matrix = lax.psum(partial_core, ('src', 'tgt')) / total_pairs]
    all_gather x0 -> x1, waiting for transfers between devices: none -> 61.1 us  [shards(): all_gather(partial_core, axis_name=('src', 'tgt')).sum(axis=0) / total_pairs]
where the time goes in v1:
time: 261 us
  blocking collectives  91.4 us (35%)
  waiting for transfers between devices  90.6 us (35%)
  other arithmetic  31.9 us (12%)
  matrix products  26.6 us (10%)
  between operations  13.7 us (5%)
  local copies, waits for them, and re-layouts  5.53 us (2%)
    all_gather x8, blocking collectives, joined(): pieces = jax.tree.map(lambda part: lax.all_gather(part, axis), value)  91.4 us
    all_gather x1, waiting for transfers between devices, shards(): all_gather(partial_core, axis_name=('src', 'tgt')).sum(axis=0) / total_pairs  61.1 us
    reduce_scatter x1, waiting for transfers between devices, shards(): lax.psum_scatter(jnp.dot(weights, target_genes, preferred_element_type=jn...  29.5 us
    dot_general x1, matrix products, shards(): lax.dot_general(left_src, geometry_right, (((0,), (0,)), ((), ())), preci...  11.4 us
    reduce_max x2, other arithmetic, row_logsum(): local_max = jnp.max(scores, axis=1)  8.87 us
    reduce_sum x2, other arithmetic, row_logsum(): local_sum = jnp.sum(jnp.exp(scores - local_max[:, None]), axis=1)  7.28 us
  transfers between devices with their start and end apart: 2, of which 2 were waited for; matrix products, arithmetic and copies ran while one was open for 2% of the time, Pallas kernels for 0%

profile of v1, /device:TPU:0, one launch (start us, length us, event | category | flops | bytes accessed | tf_op | source)
XLA Modules:
  0.0 260.6 jit_solution(4137727268448381531)
XLA Ops:
  6.5 0.0 copy-start
  6.5 0.0 all-gather.16.cloned.1.call-start
  6.5 1.1 multiply_reduce_fusion.1
  7.7 1.2 convert_element_type.20
  8.9 0.0 copy-start.6
  8.9 1.6 broadcast_multiply_fusion
  10.5 0.0 copy-start.4
  10.5 1.4 convert_element_type.19
  12.0 4.3 %fusion.21 = f32[130,4096]{1,0:T(8,128)S(1)} fusion(bf16[4096,512]{1,0:T(8,128)(2,1)S(1)} %copy-done.3, f32[128,512]{1,0:T(8,128)S(1)} %convert_element_type.20, f32[1,512]{1,0:T(1,128)S(1)} %bitcast.58, f32[1,512]{1,0:T(1,128)S(1)} %broadcast.34), kind=kOutput, calls=%fused_computation.39 | convolution fusion | flops 3271690240 | bytes 6590464 | tf_op jit(solution)/shard_map/dot_general | solution.py:68
  16.3 0.6 copy-done.5
  16.9 2.8 %fusion.18 = f32[1,130,130]{2,1,0:T(8,128)} fusion(f32[130,4096]{1,0:T(8,128)S(1)} %fusion.21, f32[128,4096]{1,0:T(8,128)S(1)} %convert_element_type.19, f32[1,4096]{1,0:T(1,128)S(1)} %bitcast.48, f32[1,4096]{1,0:T(1,128)S(1)} %broadcast.33), kind=kOutput, calls=%fused_computation.37 | convolution fusion | flops 831733760 | bytes 4327440 | tf_op jit(solution)/shard_map/dot_general | solution.py:74
  19.7 0.0 all-gather.16.cloned.1.call-update
  19.7 0.2 reduce-scatter.2.cloned.1.call-start
  19.9 4.5 %fusion.53 = f32[4096,512]{1,0:T(8,128)} fusion(bf16[128,4096]{1,0:T(8,128)(2,1)S(1)} %copy-done, bf16[128,512]{1,0:T(8,128)(2,1)S(1)} %copy-done.6), kind=kOutput, calls=%fused_computation.87 | convolution fusion | flops 536870912 | bytes 9568256 | tf_op jit(solution)/shard_map/dot_general | solution.py:88
  24.4 61.1 %all-gather.16.cloned.1.call-done = f32[32,130,130]{2,1,0:T(8,128)} async-done(((f32[1,130,130]{2,1,0:T(8,128)}), f32[32,130,130]{2,1,0:T(8,128)}) %all-gather.16.cloned.1.call-update) | async-done | bytes 2163216 | tf_op jit(solution)/shard_map/all_gather | solution.py:77
  85.5 2.6 reduce_sum.65
  88.1 0.4 fusion.27
  88.5 0.0 copy-start.8
  88.5 11.4 %fusion = (f32[512]{0:T(512)S(1)}, f32[4096,512]{1,0:T(8,128)S(1)}) fusion(f32[4096]{0:T(1024)} %param.20, f32[4096,512]{1,0:T(8,128)} %fusion.53, f32[130,512]{1,0:T(8,128)S(1)} %fusion.27, f32[128,4096]{1,0:T(8,128)S(1)} %get-tuple-element.123, f32[1,4096]{1,0:T(1,128)} %copy-done.5, f32[1,4096]{1,0:T(1,128)} %bitcast.49), kind=kOutput, calls=%fused_computation.16 | convolution fusion | flops 3285204480 | bytes 19191808 | tf_op jit(solution)/shard_map/dot_general | solution.py:81
  100.0 0.0 copy-start.1
  100.0 0.0 copy-start.9
  100.0 3.2 %copy-done.1 = f32[4096,512]{1,0:T(8,128)} copy-done((f32[4096,512]{1,0:T(8,128)}, f32[4096,512]{1,0:T(8,128)S(1)}, u32[]{:S(2)}) %copy-start.1) | copy-done | bytes 8388632
  103.2 1.8 exponential_reduce_fusion.3
  105.0 19.7 %all-gather.11 = f32[16,1,512]{2,1,0:T(1,128)S(1)} all-gather(f32[1,1,512]{2,1,0:T(1,128)S(1)} %bitcast.63), channel_id=4, replica_groups=mesh['src'=16,'tgt'=2] {'src'}, dimensions={0}, use_global_device_ids=true | all-gather | bytes 34816 | tf_op jit(solution)/shard_map/all_gather | solution.py:13
  124.7 17.5 %all-gather.10 = f32[16,1,512]{2,1,0:T(1,128)S(1)} all-gather(f32[1,1,512]{2,1,0:T(1,128)S(1)} %bitcast.60), channel_id=3, replica_groups=mesh['src'=16,'tgt'=2] {'src'}, dimensions={0}, use_global_device_ids=true | all-gather | bytes 34816 | tf_op jit(solution)/shard_map/all_gather | solution.py:13
  142.2 0.8 while.4
  143.1 0.0 copy-start.7
  143.1 4.4 %fusion.1 = f32[4096]{0:T(1024)S(1)} fusion(f32[4096,512]{1,0:T(8,128)} %copy-done.1, f32[512]{0:T(512)S(1)} %multiply_subtract_fusion.1), kind=kLoop, calls=%fused_computation.17 | loop fusion | flops 6287360 | bytes 8407040 | tf_op jit(solution)/shard_map/reduce_max | solution.py:45
  147.5 1.3 copy-done.2
  148.8 2.2 exponential_reduce_fusion.2
  151.0 4.4 %all-gather.3 = f32[8192]{0:T(1024)S(1)} all-gather(f32[4096]{0:T(1024)S(1)} %fusion.1), channel_id=5, replica_groups=mesh['src'=16,'tgt'=2] {'tgt'}, dimensions={0}, use_global_device_ids=true | all-gather | bytes 49152 | tf_op jit(solution)/shard_map/all_gather | solution.py:13
  155.4 4.4 %all-gather.4 = f32[8192]{0:T(1024)S(1)} all-gather(f32[4096]{0:T(1024)S(1)} %exponential_reduce_fusion.2), channel_id=6, replica_groups=mesh['src'=16,'tgt'=2] {'tgt'}, dimensions={0}, use_global_device_ids=true | all-gather | bytes 49152 | tf_op jit(solution)/shard_map/all_gather | solution.py:13
  159.9 1.0 fusion.2
  160.8 1.8 exponential_reduce_fusion.1
  162.7 18.9 %all-gather.13 = f32[16,1,512]{2,1,0:T(1,128)S(1)} all-gather(f32[1,1,512]{2,1,0:T(1,128)S(1)} %bitcast.62), channel_id=8, replica_groups=mesh['src'=16,'tgt'=2] {'src'}, dimensions={0}, use_global_device_ids=true | all-gather | bytes 34816 | tf_op jit(solution)/shard_map/all_gather | solution.py:13
  181.5 17.7 %all-gather.12 = f32[16,1,512]{2,1,0:T(1,128)S(1)} all-gather(f32[1,1,512]{2,1,0:T(1,128)S(1)} %bitcast.61), channel_id=7, replica_groups=mesh['src'=16,'tgt'=2] {'src'}, dimensions={0}, use_global_device_ids=true | all-gather | bytes 34816 | tf_op jit(solution)/shard_map/all_gather | solution.py:13
  199.3 0.8 while.5
  200.1 0.0 slice-start
  200.1 0.0 copy-start.10
  200.1 4.4 %fusion.3 = f32[4096]{0:T(1024)S(1)} fusion(f32[4096,512]{1,0:T(8,128)} %copy-done.1, f32[512]{0:T(512)S(1)} %multiply_subtract_fusion), kind=kLoop, calls=%fused_computation.19 | loop fusion | flops 6287360 | bytes 8407040 | tf_op jit(solution)/shard_map/reduce_max | solution.py:45
  204.5 0.0 slice-start.1
  204.6 5.1 %exponential_reduce_fusion = f32[4096]{0:T(1024)S(1)} fusion(f32[4096,512]{1,0:T(8,128)} %copy-done.1, f32[4096]{0:T(1024)S(1)} %fusion.3, f32[512]{0:T(512)S(1)} %multiply_subtract_fusion), kind=kLoop, calls=%fused_computation.7 | loop fusion | flops 8384512 | bytes 8423424 | tf_op jit(solution)/shard_map/reduce_sum | solution.py:46
  209.7 4.4 %all-gather.7 = f32[8192]{0:T(1024)S(1)} all-gather(f32[4096]{0:T(1024)S(1)} %fusion.3), channel_id=9, replica_groups=mesh['src'=16,'tgt'=2] {'tgt'}, dimensions={0}, use_global_device_ids=true | all-gather | bytes 49152 | tf_op jit(solution)/shard_map/all_gather | solution.py:13
  214.1 4.4 %all-gather.8 = f32[8192]{0:T(1024)S(1)} all-gather(f32[4096]{0:T(1024)S(1)} %exponential_reduce_fusion), channel_id=10, replica_groups=mesh['src'=16,'tgt'=2] {'tgt'}, dimensions={0}, use_global_device_ids=true | all-gather | bytes 49152 | tf_op jit(solution)/shard_map/all_gather | solution.py:13
  218.5 3.2 %convolution_convert_fusion = bf16[4096,256]{1,0:T(8,128)(2,1)} fusion(bf16[512,256]{1,0:T(8,128)(2,1)S(1)} %copy-done.10, f32[4096,512]{1,0:T(8,128)S(1)} %bitcast.43, f32[4096]{0:T(1024)S(1)} %fusion.39, f32[512]{0:T(512)S(1)} %multiply_subtract_fusion), kind=kOutput, calls=%fused_computation.20 | convolution fusion | flops 1083179008 | bytes 10766336 | tf_op jit(solution)/shard_map/dot_general | solution.py:110
  221.8 0.0 reduce-scatter.2.cloned.1.call-update
  221.8 29.5 %reduce-scatter.2.cloned.1.call-done = bf16[2048,256]{1,0:T(8,128)(2,1)} async-done(((bf16[4096,256]{1,0:T(8,128)(2,1)}), bf16[2048,256]{1,0:T(8,128)(2,1)}) %reduce-scatter.2.cloned.1.call-update) | async-done | bytes 1048592 | tf_op jit(solution)/shard_map/reduce_scatter | solution.py:109
  251.3 2.5 divide_convert_fusion
  (93 shorter events, 1.1 us)
Async XLA Ops:
  6.5 13.4 %copy-start = (bf16[128,4096]{1,0:T(8,128)(2,1)S(1)}, bf16[128,4096]{1,0:T(8,128)(2,1)}, u32[]{:S(2)}) copy-start(bf16[128,4096]{1,0:T(8,128)(2,1)} %param.15) | copy-start | bytes 3145732
  6.5 79.0 %all-gather.16.cloned.1.call-start = ((), (), s32[]{:S(2)}) async-start(), calls=%async_computation.2 | async-start | bytes 4595712 | tf_op jit(solution)/shard_map/all_gather | solution.py:77
  6.5 5.4 %copy-start.3 = (bf16[4096,512]{1,0:T(8,128)(2,1)S(1)}, bf16[4096,512]{1,0:T(8,128)(2,1)}, u32[]{:S(2)}) copy-start(bf16[4096,512]{1,0:T(8,128)(2,1)} %param.17) | copy-start | bytes 12582916
  8.9 11.0 %copy-start.6 = (bf16[128,512]{1,0:T(8,128)(2,1)S(1)}, bf16[128,512]{1,0:T(8,128)(2,1)}, u32[]{:S(2)}) copy-start(bf16[128,512]{1,0:T(8,128)(2,1)} %param.16) | copy-start | bytes 393220
  10.5 5.8 %copy-start.4 = (f32[4096]{0:T(1024)}, f32[4096]{0:T(1024)S(1)}, u32[]{:S(2)}) copy-start(f32[4096]{0:T(1024)S(1)} %get-tuple-element.124) | copy-start | bytes 49156
  16.3 0.6 copy-start.5
  19.7 231.6 %reduce-scatter.2.cloned.1.call-start = ((), (), s32[]{:S(2)}) async-start(), calls=%async_computation.1 | async-start | bytes 3145728 | tf_op jit(solution)/shard_map/reduce_scatter | solution.py:109
  88.5 14.7 %copy-start.8 = (f32[4096]{0:T(1024)S(1)}, f32[4096]{0:T(1024)}, u32[]{:S(2)}) copy-start(f32[4096]{0:T(1024)} %param.20) | copy-start | bytes 49156
  100.0 3.2 %copy-start.1 = (f32[4096,512]{1,0:T(8,128)}, f32[4096,512]{1,0:T(8,128)S(1)}, u32[]{:S(2)}) copy-start(f32[4096,512]{1,0:T(8,128)S(1)} %get-tuple-element.128) | copy-start | bytes 25165828
  100.0 43.1 %copy-start.9 = (f32[512]{0:T(512)S(1)}, f32[512]{0:T(512)}, u32[]{:S(2)}) copy-start(f32[512]{0:T(512)} %param.19) | copy-start | bytes 6148
  143.0 5.8 %copy-start.2 = (f32[4096,512]{1,0:T(8,128)S(1)}, f32[4096,512]{1,0:T(8,128)}, u32[]{:S(2)}) copy-start(f32[4096,512]{1,0:T(8,128)} %copy-done.1) | copy-start | bytes 25165828
  143.1 16.8 %copy-start.7 = (f32[4096]{0:T(1024)S(1)}, f32[4096]{0:T(1024)}, u32[]{:S(2)}) copy-start(f32[4096]{0:T(1024)} %param.18) | copy-start | bytes 49156
  200.1 18.4 %slice-start = ((s8[8388608]{0:T(1024)(128)(4,1)}), s8[4194304]{0:T(1024)(128)(4,1)S(1)}, s32[]{:S(2)}) async-start(s8[8388608]{0:T(1024)(128)(4,1)} %bitcast.42), calls=%async_computation.3 | async-start | bytes 8388608
  200.1 18.4 %copy-start.10 = (bf16[512,256]{1,0:T(8,128)(2,1)S(1)}, bf16[512,256]{1,0:T(8,128)(2,1)}, u32[]{:S(2)}) copy-start(bf16[512,256]{1,0:T(8,128)(2,1)} %param.21) | copy-start | bytes 786436
  204.5 14.0 %slice-start.1 = ((s8[8388608]{0:T(1024)(128)(4,1)}), s8[4194304]{0:T(1024)(128)(4,1)S(1)}, s32[]{:S(2)}) async-start(s8[8388608]{0:T(1024)(128)(4,1)} %bitcast.42), calls=%async_computation.4 | async-start | bytes 8388608
Sparse Core Ops, SparseCore 0:
  19.8 65.6 all-gather.15
  221.9 29.3 reduce-scatter.1
